TPU v7x, 256 devices: a whole 4x4x8 slice. The times are simulated.
256 devices in a mesh: gx: 16 (over z, x_hi), gy: 8 (over y, x_lo), gz: 2 (over core).
Axes of the slice: x: 4 (x_hi: 2, x_lo: 2; x = x_hi * 2 + x_lo), y: 4, z: 8, core: 2. Of those that a mesh axis runs over, the one named last changes fastest.
Arguments:
- forward: float32 [19, 256, 128, 256], P(None, 'gx', 'gy', 'gz'), may hold values from 0.01 to 0.15
- adjoint: float32 [19, 256, 128, 256], P(None, 'gx', 'gy', 'gz'), may hold values from -1.2 to 1.2
- design: float32 [256, 128, 256], P('gx', 'gy', 'gz'), may hold values from 0 to 1
- mask: int32 [256, 128, 256], P('gx', 'gy', 'gz'), may hold values from 0 to 3
Outputs:
- adjoint_next: float32 [19, 256, 128, 256], P(None, 'gx', 'gy', 'gz')
- sensitivity: float32 [256, 128, 256], P('gx', 'gy', 'gz')
All inputs are finite; a program needn't handle non-finite values.
Results may differ from a plain program's by a relative error of at most 0.0003.
Values sent between devices are 32-bit elements; how exact they have to be, the bound alone decides.
A program may use at most 64 MiB of HBM per device.

v0:
```python
import math

import jax
import jax.numpy as jnp
from jax import lax
from jax.sharding import PartitionSpec as P

Q = 19
RADIUS = 8


velocity = [
    (0, 0, 0),
    (1, 0, 0),
    (-1, 0, 0),
    (0, 1, 0),
    (0, -1, 0),
    (0, 0, 1),
    (0, 0, -1),
    (1, 1, 0),
    (-1, -1, 0),
    (1, -1, 0),
    (-1, 1, 0),
    (1, 0, 1),
    (-1, 0, -1),
    (1, 0, -1),
    (-1, 0, 1),
    (0, 1, 1),
    (0, -1, -1),
    (0, 1, -1),
    (0, -1, 1),
]
lattice_weight = [1.0 / 3.0] + [1.0 / 18.0] * 6 + [1.0 / 36.0] * 12
opposite = [0, 2, 1, 4, 3, 6, 5, 8, 7, 10, 9, 12, 11, 14, 13, 16, 15, 18, 17]
relax_rate = 1.25
sharpness = 64.0
threshold = 0.5
damping_max = 10.0
ramp_shape = 0.1


def extended(cells, sides, width):
    for axis, dim in sides:
        count = lax.axis_size(axis)
        ends = count - 1
        head = lax.slice_in_dim(cells, 0, width, axis=dim)
        tail = lax.slice_in_dim(cells, cells.shape[dim] - width, cells.shape[dim], axis=dim)
        cells = jnp.concatenate(
            [
                lax.ppermute(tail, axis, [(i, (i + 1) % count) for i in range(ends)]),
                cells,
                lax.ppermute(head, axis, [((i + 1) % count, i) for i in range(ends)]),
            ],
            axis=dim,
        )
    return cells


def tap_weights():
    spread_width = RADIUS / 2.0
    unscaled = [
        math.exp(-((k - RADIUS) ** 2) / (2.0 * spread_width * spread_width))
        for k in range(2 * RADIUS + 1)
    ]
    summed = sum(unscaled)
    return [v / summed for v in unscaled]


def filter_along(padded, along, length_out):
    weights = tap_weights()
    result = weights[0] * lax.slice_in_dim(padded, 0, length_out, axis=along)
    for k in range(1, 2 * RADIUS + 1):
        result = result + weights[k] * lax.slice_in_dim(padded, k, k + length_out, axis=along)
    return result


def smooth(field):
    extent = field.shape
    padded = extended(field, (("gx", 0),), RADIUS)
    field = filter_along(padded, 0, extent[0])
    padded = extended(field, (("gy", 1),), RADIUS)
    field = filter_along(padded, 1, extent[1])
    padded = extended(field, (("gz", 2),), RADIUS)
    field = filter_along(padded, 2, extent[2])
    return field


def project(filtered):
    base = math.tanh(sharpness * threshold)
    denominator = base + math.tanh(sharpness * (1.0 - threshold))
    inner = jnp.tanh(sharpness * (filtered - threshold))
    physical = (base + inner) / denominator
    steep = sharpness * (1.0 - inner * inner) / denominator
    return (physical, steep)


def ramp(physical):
    damping = damping_max * ramp_shape * (1.0 - physical) / (ramp_shape + physical)
    slope = (
        -damping_max
        * ramp_shape
        * (1.0 + ramp_shape)
        / ((ramp_shape + physical) * (ramp_shape + physical))
    )
    return (damping, slope)


def weighted_sum(members, factors):
    result = None
    for member, factor in zip(members, factors):
        if factor == 0:
            continue
        addend = factor * member
        result = addend if result is None else result + addend
    return result


def collide(pulled, forward, mask, damping, slope):
    forward_list = [forward[q] for q in range(Q)]
    density = weighted_sum(forward_list, [1.0] * Q)
    vel = [weighted_sum(forward_list, [float(d[a]) for d in velocity]) / density for a in range(3)]
    speed_sq = vel[0] * vel[0] + vel[1] * vel[1] + vel[2] * vel[2]
    zeroth = weighted_sum(pulled, lattice_weight)
    first = [
        weighted_sum(pulled, [w * d[a] for w, d in zip(lattice_weight, velocity)]) for a in range(3)
    ]
    second = [
        [
            weighted_sum(pulled, [w * d[a] * d[b] for w, d in zip(lattice_weight, velocity)])
            for b in range(3)
        ]
        for a in range(3)
    ]
    quadric = None
    for a in range(3):
        for b in range(3):
            addend = vel[a] * vel[b] * second[a][b]
            quadric = addend if quadric is None else quadric + addend
    eq_scalar = zeroth * (1.0 + 1.5 * speed_sq) - 4.5 * quadric
    eq_vector = [
        3.0 * first[a]
        + 9.0 * (second[a][0] * vel[0] + second[a][1] * vel[1] + second[a][2] * vel[2])
        - 3.0 * zeroth * vel[a]
        for a in range(3)
    ]
    moment = [weighted_sum(pulled, [float(d[a]) for d in velocity]) for a in range(3)]
    source = slope * (speed_sq - (vel[0] * moment[0] + vel[1] * moment[1] + vel[2] * moment[2]))
    outputs = []
    for q in range(Q):
        step_dir = velocity[q]
        along_eq = eq_scalar
        along_vel = 0.0
        for a in range(3):
            if step_dir[a] != 0:
                along_eq = along_eq + step_dir[a] * eq_vector[a]
                along_vel = along_vel + step_dir[a] * vel[a]
        own = pulled[q]
        fluid = (
            (1.0 - relax_rate) * own
            + relax_rate * along_eq
            + 2.0 * damping * (along_vel - speed_sq) / density
        )
        solid = pulled[opposite[q]]
        value = jnp.where(
            mask == 0, fluid, jnp.where(mask == 1, solid, jnp.where(mask == 2, along_eq, eq_scalar))
        )
        outputs.append(value)
    return (jnp.stack(outputs), source)


def local(forward, adjoint, design, mask):
    filtered = smooth(design)
    physical, steep = project(filtered)
    damping, slope = ramp(physical)
    extent = adjoint.shape[1:]
    padded = extended(adjoint, (("gx", 1), ("gy", 2), ("gz", 3)), 1)
    pulled = []
    for q in range(Q):
        step_dir = velocity[q]
        begin = (1 + step_dir[0], 1 + step_dir[1], 1 + step_dir[2])
        pulled.append(
            lax.slice(
                padded[q], begin, (begin[0] + extent[0], begin[1] + extent[1], begin[2] + extent[2])
            )
        )
    adjoint_next, source = collide(pulled, forward, mask, damping, slope)
    sensitivity = smooth(steep * source)
    return (adjoint_next, sensitivity)


def solution(mesh):
    return jax.shard_map(
        local,
        mesh=mesh,
        in_specs=(
            P(None, "gx", "gy", "gz"),
            P(None, "gx", "gy", "gz"),
            P("gx", "gy", "gz"),
            P("gx", "gy", "gz"),
        ),
        out_specs=(P(None, "gx", "gy", "gz"), P("gx", "gy", "gz")),
        check_vma=False,
    )
```

profile of v0, /device:TPU:109, one launch (start us, length us, event | category | flops | bytes accessed | tf_op | source)
XLA Modules:
  0.0 124.4 jit_solution(2331135996737809231)
XLA Ops:
  1.7 4.7 %collective-permute-start.6 = (f32[8,16,128]{2,1,0:T(8,128)S(1)}, f32[8,16,128]{2,1,0:T(8,128)S(1)}, u32[]{:S(2)}, u32[]{:S(2)}) collective-permute-start(f32[8,16,128]{2,1,0:T(8,128)S(1)} %get-tuple-element.58), channel_id=1, source_target_pairs={{0,16},{16,32},{32,48},{48,64},{64,80},{80,96},{96,112},{112,128},... | collective-permute-start | bytes 196616 | tf_op jit(solution)/shard_map/ppermute | solution.py:50
  7.4 4.7 %collective-permute-start = (f32[19,1,16,128]{3,2,1,0:T(8,128)S(1)}, f32[19,1,16,128]{3,2,1,0:T(8,128)S(1)}, u32[]{:S(2)}, u32[]{:S(2)}) collective-permute-start(f32[19,1,16,128]{3,2,1,0:T(8,128)S(1)} %get-tuple-element.45), channel_id=1, source_target_pairs={{0,16},{16,32},{32,48},{48,64},{64,80},{80,96},{96,112},{112,128},... | collective-permute-start | bytes 466952 | tf_op jit(solution)/shard_map/ppermute | solution.py:50
  12.1 2.1 %collective-permute-start.1 = (f32[19,1,16,128]{3,2,1,0:T(8,128)S(1)}, f32[19,1,16,128]{3,2,1,0:T(8,128)S(1)}, u32[]{:S(2)}, u32[]{:S(2)}) collective-permute-start(f32[19,1,16,128]{3,2,1,0:T(8,128)S(1)} %get-tuple-element.44), channel_id=1, source_target_pairs={{16,0},{32,16},{48,32},{64,48},{80,64},{96,80},{112,96},{128,112},... | collective-permute-start | bytes 466952 | tf_op jit(solution)/shard_map/ppermute | solution.py:52
  14.2 3.0 %collective-permute-start.7 = (f32[8,16,128]{2,1,0:T(8,128)S(1)}, f32[8,16,128]{2,1,0:T(8,128)S(1)}, u32[]{:S(2)}, u32[]{:S(2)}) collective-permute-start(f32[8,16,128]{2,1,0:T(8,128)S(1)} %get-tuple-element.59), channel_id=1, source_target_pairs={{16,0},{32,16},{48,32},{64,48},{80,64},{96,80},{112,96},{128,112},... | collective-permute-start | bytes 196616 | tf_op jit(solution)/shard_map/ppermute | solution.py:52
  18.2 5.7 %collective-permute-done.7 = f32[8,16,128]{2,1,0:T(8,128)S(1)} collective-permute-done((f32[8,16,128]{2,1,0:T(8,128)S(1)}, f32[8,16,128]{2,1,0:T(8,128)S(1)}, u32[]{:S(2)}, u32[]{:S(2)}) %collective-permute-start.7) | collective-permute-done | bytes 65568 | tf_op jit(solution)/shard_map/ppermute | solution.py:52
  24.9 3.1 %collective-permute-start.8 = (f32[16,8,128]{2,1,0:T(8,128)S(1)}, f32[16,8,128]{2,1,0:T(8,128)S(1)}, u32[]{:S(2)}, u32[]{:S(2)}) collective-permute-start(f32[16,8,128]{2,1,0:T(8,128)S(1)} %get-tuple-element.54), channel_id=1, source_target_pairs={{0,2},{2,4},{4,6},{6,8},{8,10},{10,12},{12,14},{1,3},{3,5},{5,7},{... | collective-permute-start | bytes 196616 | tf_op jit(solution)/shard_map/ppermute | solution.py:50
  28.0 3.1 %collective-permute-start.9 = (f32[16,8,128]{2,1,0:T(8,128)S(1)}, f32[16,8,128]{2,1,0:T(8,128)S(1)}, u32[]{:S(2)}, u32[]{:S(2)}) collective-permute-start(f32[16,8,128]{2,1,0:T(8,128)S(1)} %get-tuple-element.55), channel_id=1, source_target_pairs={{2,0},{4,2},{6,4},{8,6},{10,8},{12,10},{14,12},{3,1},{5,3},{7,5},{... | collective-permute-start | bytes 196616 | tf_op jit(solution)/shard_map/ppermute | solution.py:52
  31.7 2.2 %collective-permute-start.2 = (f32[19,18,1,128]{3,2,1,0:T(1,128)S(1)}, f32[19,18,1,128]{3,2,1,0:T(1,128)S(1)}, u32[]{:S(2)}, u32[]{:S(2)}) collective-permute-start(f32[19,18,1,128]{3,2,1,0:T(1,128)S(1)} %get-tuple-element.42), channel_id=1, source_target_pairs={{0,2},{2,4},{4,6},{6,8},{8,10},{10,12},{12,14},{1,3},{3,5},{5,7},{... | collective-permute-start | bytes 525320 | tf_op jit(solution)/shard_map/ppermute | solution.py:50
  33.8 4.0 %collective-permute-start.3 = (f32[19,18,1,128]{3,2,1,0:T(1,128)S(1)}, f32[19,18,1,128]{3,2,1,0:T(1,128)S(1)}, u32[]{:S(2)}, u32[]{:S(2)}) collective-permute-start(f32[19,18,1,128]{3,2,1,0:T(1,128)S(1)} %get-tuple-element.43), channel_id=1, source_target_pairs={{2,0},{4,2},{6,4},{8,6},{10,8},{12,10},{14,12},{3,1},{5,3},{7,5},{... | collective-permute-start | bytes 525320 | tf_op jit(solution)/shard_map/ppermute | solution.py:52
  38.8 3.4 %collective-permute-done.3 = f32[19,18,1,128]{3,2,1,0:T(1,128)S(1)} collective-permute-done((f32[19,18,1,128]{3,2,1,0:T(1,128)S(1)}, f32[19,18,1,128]{3,2,1,0:T(1,128)S(1)}, u32[]{:S(2)}, u32[]{:S(2)}) %collective-permute-start.3) | collective-permute-done | bytes 175136 | tf_op jit(solution)/shard_map/ppermute | solution.py:52
  42.9 4.6 %fusion.284 = (f32[19,18,18,1]{3,2,1,0:T(8,128)}, f32[19,18,18,1]{3,2,1,0:T(8,128)}) fusion(f32[19,18,18,128]{3,2,1,0:T(8,128)S(1)} %pad_maximum_fusion.1), kind=kLoop, calls=%fused_computation.543 | loop fusion | bytes 98496 | tf_op jit(solution)/shard_map/slice | solution.py:47
  47.5 3.7 %copy.27 = f32[19,18,18,1]{0,3,2,1:T(1,128)S(1)} copy(f32[19,18,18,1]{3,2,1,0:T(8,128)} %get-tuple-element.40) | data formatting | bytes 49248 | tf_op jit(solution)/shard_map/slice | solution.py:47
  52.5 4.3 %copy.28 = f32[19,18,18,1]{0,3,2,1:T(1,128)} copy(f32[19,18,18,1]{3,2,1,0:T(8,128)} %get-tuple-element.41) | data formatting | bytes 49248 | tf_op jit(solution)/shard_map/slice | solution.py:46
  56.8 6.3 %collective-permute-start.5 = (f32[19,18,18,1]{0,3,2,1:T(1,128)}, f32[19,18,18,1]{0,3,2,1:T(1,128)}, u32[]{:S(2)}, u32[]{:S(2)}) collective-permute-start(f32[19,18,18,1]{0,3,2,1:T(1,128)} %copy.28), channel_id=1, source_target_pairs={{1,0},{3,2},{5,4},{7,6},{9,8},{11,10},{13,12},{15,14},{17,16},{19,... | collective-permute-start | bytes 73880 | tf_op jit(solution)/shard_map/ppermute | solution.py:52
  65.1 4.3 %collective-permute-start.11 = (f32[16,16,8]{2,1,0:T(8,128)}, f32[16,16,8]{2,1,0:T(8,128)}, u32[]{:S(2)}, u32[]{:S(2)}) collective-permute-start(f32[16,16,8]{2,1,0:T(8,128)} %get-tuple-element.53), channel_id=1, source_target_pairs={{1,0},{3,2},{5,4},{7,6},{9,8},{11,10},{13,12},{15,14},{17,16},{19,... | collective-permute-start | bytes 24584 | tf_op jit(solution)/shard_map/ppermute | solution.py:52
  69.5 5.0 %copy.29 = f32[19,18,18,1]{3,2,1,0:T(8,128)} copy(f32[19,18,18,1]{0,3,2,1:T(1,128)} %collective-permute-done.4) | data formatting | bytes 49248 | tf_op jit(solution)/shard_map/ppermute | solution.py:50
  74.5 5.0 %copy.30 = f32[19,18,18,1]{3,2,1,0:T(8,128)} copy(f32[19,18,18,1]{0,3,2,1:T(1,128)} %collective-permute-done.5) | data formatting | bytes 49248 | tf_op jit(solution)/shard_map/ppermute | solution.py:52
  79.5 8.4 %pad_maximum_fusion = f32[19,18,18,130]{3,2,1,0:T(8,128)S(1)} fusion(f32[19,18,18,1]{3,2,1,0:T(8,128)} %copy.30, f32[19,18,1,128]{3,2,1,0:T(1,128)S(1)} %collective-permute-done.3, f32[19,18,16,128]{3,2,1,0:T(8,128)S(1)} %constant_dynamic-update-slice_fusion, f32[19,18,1,128]{3,2,1,0:T(1,128)S(1)} %collective-permute-done.2, f32[19,18,18,1]{3,2,1,0:T(8,128)} %copy.29), kind=kLoop, calls=%fused_computation | loop fusion | flops 3201120 | bytes 6402240 | tf_op jit(solution)/shard_map/concatenate | solution.py:48
  89.6 3.7 %multiply_multiply_fusion = (f32[16,16,128]{2,1,0:T(8,128)S(1)}, f32[16,16,128]{2,1,0:T(8,128)S(1)}, f32[16,16,128]{2,1,0:T(8,128)S(1)}, f32[16,16,128]{2,1,0:T(...) fusion(f32[18,18,130]{2,1,0:T(8,128)S(1)} %get-tuple-element.25, ...), kind=kLoop, calls=%fused_computation.515 | loop fusion | flops 5603328 | bytes 5914624 | tf_op jit(solution)/shard_map/mul | solution.py:187
  93.3 3.7 %collective-permute-start.12 = (f32[8,16,128]{2,1,0:T(8,128)S(1)}, f32[8,16,128]{2,1,0:T(8,128)S(1)}, u32[]{:S(2)}, u32[]{:S(2)}) collective-permute-start(f32[8,16,128]{2,1,0:T(8,128)S(1)} %get-tuple-element.50), channel_id=1, source_target_pairs={{0,16},{16,32},{32,48},{48,64},{64,80},{80,96},{96,112},{112,128},... | collective-permute-start | bytes 196616 | tf_op jit(solution)/shard_map/ppermute | solution.py:50
  97.0 3.1 %collective-permute-start.13 = (f32[8,16,128]{2,1,0:T(8,128)S(1)}, f32[8,16,128]{2,1,0:T(8,128)S(1)}, u32[]{:S(2)}, u32[]{:S(2)}) collective-permute-start(f32[8,16,128]{2,1,0:T(8,128)S(1)} %get-tuple-element.51), channel_id=1, source_target_pairs={{16,0},{32,16},{48,32},{64,48},{80,64},{96,80},{112,96},{128,112},... | collective-permute-start | bytes 196616 | tf_op jit(solution)/shard_map/ppermute | solution.py:52
  106.1 5.1 %collective-permute-start.14 = (f32[16,8,128]{2,1,0:T(8,128)S(1)}, f32[16,8,128]{2,1,0:T(8,128)S(1)}, u32[]{:S(2)}, u32[]{:S(2)}) collective-permute-start(f32[16,8,128]{2,1,0:T(8,128)S(1)} %get-tuple-element.48), channel_id=1, source_target_pairs={{0,2},{2,4},{4,6},{6,8},{8,10},{10,12},{12,14},{1,3},{3,5},{5,7},{... | collective-permute-start | bytes 196616 | tf_op jit(solution)/shard_map/ppermute | solution.py:50
  113.4 2.9 %collective-permute-done.15 = f32[16,8,128]{2,1,0:T(8,128)S(1)} collective-permute-done((f32[16,8,128]{2,1,0:T(8,128)S(1)}, f32[16,8,128]{2,1,0:T(8,128)S(1)}, u32[]{:S(2)}, u32[]{:S(2)}) %collective-permute-start.15) | collective-permute-done | bytes 65568 | tf_op jit(solution)/shard_map/ppermute | solution.py:52
  118.0 3.7 %collective-permute-start.17 = (f32[16,16,8]{2,1,0:T(8,128)S(1)}, f32[16,16,8]{2,1,0:T(8,128)S(1)}, u32[]{:S(2)}, u32[]{:S(2)}) collective-permute-start(f32[16,16,8]{2,1,0:T(8,128)S(1)} %get-tuple-element.47), channel_id=1, source_target_pairs={{1,0},{3,2},{5,4},{7,6},{9,8},{11,10},{13,12},{15,14},{17,16},{19,... | collective-permute-start | bytes 24584 | tf_op jit(solution)/shard_map/ppermute | solution.py:52
  (67 shorter events, 23.6 us)
Async XLA Ops:
  0.6 30.5 %copy-start = (f32[19,16,16,128]{3,2,1,0:T(8,128)S(1)}, f32[19,16,16,128]{3,2,1,0:T(8,128)}, u32[]{:S(2)}) copy-start(f32[19,16,16,128]{3,2,1,0:T(8,128)} %param.5) | copy-start | bytes 7471108
  1.7 15.5 %collective-permute-start.6 = (f32[8,16,128]{2,1,0:T(8,128)S(1)}, f32[8,16,128]{2,1,0:T(8,128)S(1)}, u32[]{:S(2)}, u32[]{:S(2)}) collective-permute-start(f32[8,16,128]{2,1,0:T(8,128)S(1)} %get-tuple-element.58), channel_id=1, source_target_pairs={{0,16},{16,32},{32,48},{48,64},{64,80},{80,96},{96,112},{112,128},... | collective-permute-start | bytes 196616 | tf_op jit(solution)/shard_map/ppermute | solution.py:50
  7.4 23.7 %collective-permute-start = (f32[19,1,16,128]{3,2,1,0:T(8,128)S(1)}, f32[19,1,16,128]{3,2,1,0:T(8,128)S(1)}, u32[]{:S(2)}, u32[]{:S(2)}) collective-permute-start(f32[19,1,16,128]{3,2,1,0:T(8,128)S(1)} %get-tuple-element.45), channel_id=1, source_target_pairs={{0,16},{16,32},{32,48},{48,64},{64,80},{80,96},{96,112},{112,128},... | collective-permute-start | bytes 466952 | tf_op jit(solution)/shard_map/ppermute | solution.py:50
  12.1 19.3 %collective-permute-start.1 = (f32[19,1,16,128]{3,2,1,0:T(8,128)S(1)}, f32[19,1,16,128]{3,2,1,0:T(8,128)S(1)}, u32[]{:S(2)}, u32[]{:S(2)}) collective-permute-start(f32[19,1,16,128]{3,2,1,0:T(8,128)S(1)} %get-tuple-element.44), channel_id=1, source_target_pairs={{16,0},{32,16},{48,32},{64,48},{80,64},{96,80},{112,96},{128,112},... | collective-permute-start | bytes 466952 | tf_op jit(solution)/shard_map/ppermute | solution.py:52
  14.2 9.6 %collective-permute-start.7 = (f32[8,16,128]{2,1,0:T(8,128)S(1)}, f32[8,16,128]{2,1,0:T(8,128)S(1)}, u32[]{:S(2)}, u32[]{:S(2)}) collective-permute-start(f32[8,16,128]{2,1,0:T(8,128)S(1)} %get-tuple-element.59), channel_id=1, source_target_pairs={{16,0},{32,16},{48,32},{64,48},{80,64},{96,80},{112,96},{128,112},... | collective-permute-start | bytes 196616 | tf_op jit(solution)/shard_map/ppermute | solution.py:52
  24.9 13.0 %collective-permute-start.8 = (f32[16,8,128]{2,1,0:T(8,128)S(1)}, f32[16,8,128]{2,1,0:T(8,128)S(1)}, u32[]{:S(2)}, u32[]{:S(2)}) collective-permute-start(f32[16,8,128]{2,1,0:T(8,128)S(1)} %get-tuple-element.54), channel_id=1, source_target_pairs={{0,2},{2,4},{4,6},{6,8},{8,10},{10,12},{12,14},{1,3},{3,5},{5,7},{... | collective-permute-start | bytes 196616 | tf_op jit(solution)/shard_map/ppermute | solution.py:50
  28.0 9.9 %collective-permute-start.9 = (f32[16,8,128]{2,1,0:T(8,128)S(1)}, f32[16,8,128]{2,1,0:T(8,128)S(1)}, u32[]{:S(2)}, u32[]{:S(2)}) collective-permute-start(f32[16,8,128]{2,1,0:T(8,128)S(1)} %get-tuple-element.55), channel_id=1, source_target_pairs={{2,0},{4,2},{6,4},{8,6},{10,8},{12,10},{14,12},{3,1},{5,3},{7,5},{... | collective-permute-start | bytes 196616 | tf_op jit(solution)/shard_map/ppermute | solution.py:52
  31.7 7.1 %collective-permute-start.2 = (f32[19,18,1,128]{3,2,1,0:T(1,128)S(1)}, f32[19,18,1,128]{3,2,1,0:T(1,128)S(1)}, u32[]{:S(2)}, u32[]{:S(2)}) collective-permute-start(f32[19,18,1,128]{3,2,1,0:T(1,128)S(1)} %get-tuple-element.42), channel_id=1, source_target_pairs={{0,2},{2,4},{4,6},{6,8},{8,10},{10,12},{12,14},{1,3},{3,5},{5,7},{... | collective-permute-start | bytes 525320 | tf_op jit(solution)/shard_map/ppermute | solution.py:50
  33.8 8.4 %collective-permute-start.3 = (f32[19,18,1,128]{3,2,1,0:T(1,128)S(1)}, f32[19,18,1,128]{3,2,1,0:T(1,128)S(1)}, u32[]{:S(2)}, u32[]{:S(2)}) collective-permute-start(f32[19,18,1,128]{3,2,1,0:T(1,128)S(1)} %get-tuple-element.43), channel_id=1, source_target_pairs={{2,0},{4,2},{6,4},{8,6},{10,8},{12,10},{14,12},{3,1},{5,3},{7,5},{... | collective-permute-start | bytes 525320 | tf_op jit(solution)/shard_map/ppermute | solution.py:52
  51.2 18.3 %collective-permute-start.4 = (f32[19,18,18,1]{0,3,2,1:T(1,128)S(1)}, f32[19,18,18,1]{0,3,2,1:T(1,128)}, u32[]{:S(2)}, u32[]{:S(2)}) collective-permute-start(f32[19,18,18,1]{0,3,2,1:T(1,128)S(1)} %copy.27), channel_id=1, source_target_pairs={{0,1},{2,3},{4,5},{6,7},{8,9},{10,11},{12,13},{14,15},{16,17},{18,... | collective-permute-start | bytes 73880 | tf_op jit(solution)/shard_map/ppermute | solution.py:50
  56.8 17.7 %collective-permute-start.5 = (f32[19,18,18,1]{0,3,2,1:T(1,128)}, f32[19,18,18,1]{0,3,2,1:T(1,128)}, u32[]{:S(2)}, u32[]{:S(2)}) collective-permute-start(f32[19,18,18,1]{0,3,2,1:T(1,128)} %copy.28), channel_id=1, source_target_pairs={{1,0},{3,2},{5,4},{7,6},{9,8},{11,10},{13,12},{15,14},{17,16},{19,... | collective-permute-start | bytes 73880 | tf_op jit(solution)/shard_map/ppermute | solution.py:52
  63.8 24.7 %collective-permute-start.10 = (f32[16,16,8]{2,1,0:T(8,128)}, f32[16,16,8]{2,1,0:T(8,128)}, u32[]{:S(2)}, u32[]{:S(2)}) collective-permute-start(f32[16,16,8]{2,1,0:T(8,128)} %get-tuple-element.52), channel_id=1, source_target_pairs={{0,1},{2,3},{4,5},{6,7},{8,9},{10,11},{12,13},{14,15},{16,17},{18,... | collective-permute-start | bytes 24584 | tf_op jit(solution)/shard_map/ppermute | solution.py:50
  65.1 23.4 %collective-permute-start.11 = (f32[16,16,8]{2,1,0:T(8,128)}, f32[16,16,8]{2,1,0:T(8,128)}, u32[]{:S(2)}, u32[]{:S(2)}) collective-permute-start(f32[16,16,8]{2,1,0:T(8,128)} %get-tuple-element.53), channel_id=1, source_target_pairs={{1,0},{3,2},{5,4},{7,6},{9,8},{11,10},{13,12},{15,14},{17,16},{19,... | collective-permute-start | bytes 24584 | tf_op jit(solution)/shard_map/ppermute | solution.py:52
  87.9 1.7 %copy-start.1 = (f32[19,16,16,128]{3,2,1,0:T(8,128)S(1)}, f32[19,16,16,128]{3,2,1,0:T(8,128)}, u32[]{:S(2)}) copy-start(f32[19,16,16,128]{3,2,1,0:T(8,128)} %param.4) | copy-start | bytes 7471108
  89.6 10.5 %copy-start.2 = (s32[16,16,128]{2,1,0:T(8,128)S(1)}, s32[16,16,128]{2,1,0:T(8,128)}, u32[]{:S(2)}) copy-start(s32[16,16,128]{2,1,0:T(8,128)} %param.7) | copy-start | bytes 393220
  93.3 11.7 %collective-permute-start.12 = (f32[8,16,128]{2,1,0:T(8,128)S(1)}, f32[8,16,128]{2,1,0:T(8,128)S(1)}, u32[]{:S(2)}, u32[]{:S(2)}) collective-permute-start(f32[8,16,128]{2,1,0:T(8,128)S(1)} %get-tuple-element.50), channel_id=1, source_target_pairs={{0,16},{16,32},{32,48},{48,64},{64,80},{80,96},{96,112},{112,128},... | collective-permute-start | bytes 196616 | tf_op jit(solution)/shard_map/ppermute | solution.py:50
  97.0 9.0 %collective-permute-start.13 = (f32[8,16,128]{2,1,0:T(8,128)S(1)}, f32[8,16,128]{2,1,0:T(8,128)S(1)}, u32[]{:S(2)}, u32[]{:S(2)}) collective-permute-start(f32[8,16,128]{2,1,0:T(8,128)S(1)} %get-tuple-element.51), channel_id=1, source_target_pairs={{16,0},{32,16},{48,32},{64,48},{80,64},{96,80},{112,96},{128,112},... | collective-permute-start | bytes 196616 | tf_op jit(solution)/shard_map/ppermute | solution.py:52
  106.1 7.2 %collective-permute-start.14 = (f32[16,8,128]{2,1,0:T(8,128)S(1)}, f32[16,8,128]{2,1,0:T(8,128)S(1)}, u32[]{:S(2)}, u32[]{:S(2)}) collective-permute-start(f32[16,8,128]{2,1,0:T(8,128)S(1)} %get-tuple-element.48), channel_id=1, source_target_pairs={{0,2},{2,4},{4,6},{6,8},{8,10},{10,12},{12,14},{1,3},{3,5},{5,7},{... | collective-permute-start | bytes 196616 | tf_op jit(solution)/shard_map/ppermute | solution.py:50
  111.2 5.0 %collective-permute-start.15 = (f32[16,8,128]{2,1,0:T(8,128)S(1)}, f32[16,8,128]{2,1,0:T(8,128)S(1)}, u32[]{:S(2)}, u32[]{:S(2)}) collective-permute-start(f32[16,8,128]{2,1,0:T(8,128)S(1)} %get-tuple-element.49), channel_id=1, source_target_pairs={{2,0},{4,2},{6,4},{8,6},{10,8},{12,10},{14,12},{3,1},{5,3},{7,5},{... | collective-permute-start | bytes 196616 | tf_op jit(solution)/shard_map/ppermute | solution.py:52
  116.7 5.2 %collective-permute-start.16 = (f32[16,16,8]{2,1,0:T(8,128)S(1)}, f32[16,16,8]{2,1,0:T(8,128)S(1)}, u32[]{:S(2)}, u32[]{:S(2)}) collective-permute-start(f32[16,16,8]{2,1,0:T(8,128)S(1)} %get-tuple-element.46), channel_id=1, source_target_pairs={{0,1},{2,3},{4,5},{6,7},{8,9},{10,11},{12,13},{14,15},{16,17},{18,... | collective-permute-start | bytes 24584 | tf_op jit(solution)/shard_map/ppermute | solution.py:50
  118.0 4.7 %collective-permute-start.17 = (f32[16,16,8]{2,1,0:T(8,128)S(1)}, f32[16,16,8]{2,1,0:T(8,128)S(1)}, u32[]{:S(2)}, u32[]{:S(2)}) collective-permute-start(f32[16,16,8]{2,1,0:T(8,128)S(1)} %get-tuple-element.47), channel_id=1, source_target_pairs={{1,0},{3,2},{5,4},{7,6},{9,8},{11,10},{13,12},{15,14},{17,16},{19,... | collective-permute-start | bytes 24584 | tf_op jit(solution)/shard_map/ppermute | solution.py:52
  121.9 2.5 %copy-start.3 = (f32[19,16,16,128]{3,2,1,0:T(8,128)}, f32[19,16,16,128]{3,2,1,0:T(8,128)S(1)}, u32[]{:S(2)}) copy-start(f32[19,16,16,128]{3,2,1,0:T(8,128)S(1)} %bitcast_dynamic-update-slice_fusion) | copy-start | bytes 7471108
where the time goes:
time: 125 us; the launch traced here: 124 us
  starting transfers between devices  58.8 us (47%)
  local copies, waits for them, and re-layouts  28.7 us (23%)
  other arithmetic  21.6 us (17%)
  waiting for transfers between devices  14.2 us (11%)
    ppermute x9, starting transfers between devices, extended(): lax.ppermute(head, axis, [((i + 1) % count, i) for i in range(ends)])  31.6 us
    ppermute x9, starting transfers between devices, extended(): lax.ppermute(tail, axis, [(i, (i + 1) % count) for i in range(ends)])  27.2 us
    ppermute x9, waiting for transfers between devices, extended(): lax.ppermute(head, axis, [((i + 1) % count, i) for i in range(ends)])  13.7 us
    slice x9, local copies, waits for them, and re-layouts, extended(): lax.slice_in_dim(cells, cells.shape[dim] - width, cells.shape[dim], axis=...  10.5 us
    concatenate x2, other arithmetic, extended(): jnp.concatenate([lax.ppermute(tail, axis, [(i, (i + 1) % count) for i in...  9.06 us
    slice x2, local copies, waits for them, and re-layouts, extended(): head = lax.slice_in_dim(cells, 0, width, axis=dim)  5.34 us
    unnamed x18, other arithmetic  5.03 us
    ppermute x1, local copies, waits for them, and re-layouts, extended(): lax.ppermute(tail, axis, [(i, (i + 1) % count) for i in range(ends)])  5.02 us
  transfers between devices with their start and end apart: 18, of which 6 were waited for; matrix products, arithmetic and copies ran while one was open for 27% of the time, Pallas kernels for 0%

commit v1 on v0

v1 whole, which is shorter than its diff:
```python
import functools
import math

import jax
import jax.numpy as jnp
from jax import lax
from jax.experimental import pallas as pl
from jax.experimental.pallas import tpu as pltpu
from jax.sharding import PartitionSpec as P

Q = 19
RADIUS = 8
MESH = pl.DeviceIdType.MESH
F32 = jnp.float32

velocity = [
    (0, 0, 0),
    (1, 0, 0),
    (-1, 0, 0),
    (0, 1, 0),
    (0, -1, 0),
    (0, 0, 1),
    (0, 0, -1),
    (1, 1, 0),
    (-1, -1, 0),
    (1, -1, 0),
    (-1, 1, 0),
    (1, 0, 1),
    (-1, 0, -1),
    (1, 0, -1),
    (-1, 0, 1),
    (0, 1, 1),
    (0, -1, -1),
    (0, 1, -1),
    (0, -1, 1),
]
lattice_weight = [1.0 / 3.0] + [1.0 / 18.0] * 6 + [1.0 / 36.0] * 12
opposite = [0, 2, 1, 4, 3, 6, 5, 8, 7, 10, 9, 12, 11, 14, 13, 16, 15, 18, 17]
relax_rate = 1.25
sharpness = 64.0
threshold = 0.5
damping_max = 10.0
ramp_shape = 0.1

slot_of = {5: 0, 6: 0, 11: 1, 12: 1, 14: 2, 13: 2, 15: 3, 16: 3, 18: 4, 17: 4}

unscaled = [math.exp(-(k * k) / (2.0 * (RADIUS / 2.0) ** 2)) for k in range(RADIUS + 1)]
tap_sum = unscaled[0] + 2.0 * sum(unscaled[1:])
TAPS = [v / tap_sum for v in unscaled]


def tap_matrix(offset):
    row = lax.broadcasted_iota(jnp.int32, (128, 128), 0)
    col = lax.broadcasted_iota(jnp.int32, (128, 128), 1)
    gap = jnp.abs(row + offset - col)
    result = jnp.zeros((128, 128), F32)
    for k in range(RADIUS + 1):
        result = jnp.where(gap == k, TAPS[k], result)
    return result


def symmetric(take):
    total = TAPS[0] * take(0)
    for k in range(1, RADIUS + 1):
        total = total + TAPS[k] * (take(k) + take(-k))
    return total


def filter_xy(source, middle, result):
    def along_x(group, carry):
        rows = pl.ds(pl.multiple_of(group * 8, 8), 8)
        planes = [source[i, rows, :] for i in range(32)]
        for i in range(16):
            middle[i, rows, :] = symmetric(lambda k: planes[i + 8 + k])
        return carry

    lax.fori_loop(0, 4, along_x, 0)

    def along_y(i, carry):
        for half in range(2):
            at = 8 + 8 * half
            result[i, pl.ds(8 * half, 8), :] = symmetric(
                lambda k: middle[i, pl.ds(at + k, 8), :]
            )
        return carry

    lax.fori_loop(0, 16, along_y, 0)


def dot(a, b):
    return jnp.dot(a, b, precision=lax.Precision.HIGHEST, preferred_element_type=F32)


def add_all(members):
    total = None
    for sign, member in members:
        if total is None:
            total = member if sign > 0 else -member
        else:
            total = total + member if sign > 0 else total - member
    return total


def main_kernel(
    forward,
    adjoint,
    design,
    mask,
    out,
    grad,
    padded,
    beside,
    flow,
    label,
    field,
    middle,
    smoothed,
    smoothed_beside,
    motion,
    chain,
    damp,
    raw,
    raw_beside,
    local_sem,
    send_sem,
    recv_sem,
):
    nx, ny = lax.axis_size("gx"), lax.axis_size("gy")
    X, Y, Z = lax.axis_index("gx"), lax.axis_index("gy"), lax.axis_index("gz")
    low_x, high_x = X > 0, X < nx - 1
    low_y, high_y = Y > 0, Y < ny - 1

    def exists(dx, dy):
        found = True
        if dx:
            found = high_x if dx > 0 else low_x
        if dy:
            found_y = high_y if dy > 0 else low_y
            found = found_y if found is True else jnp.logical_and(found, found_y)
        return found

    def when(cond, body):
        if cond is True:
            body()
        else:
            pl.when(cond)(body)

    def device(dx, dy, other):
        return (X + dx, Y + dy, 1 - Z if other else Z)

    loads = [
        pltpu.make_async_copy(design, field.at[8:24, 8:24, :], local_sem.at[0]),
        pltpu.make_async_copy(forward, flow, local_sem.at[1]),
        pltpu.make_async_copy(adjoint, padded.at[:, 1:17, 8:24, :], local_sem.at[2]),
        pltpu.make_async_copy(mask, label, local_sem.at[3]),
    ]
    for load in loads:
        load.start()

    around = [(dx, dy, 0) for dx in (-1, 0, 1) for dy in (-1, 0, 1) if dx or dy]
    around += [(0, 0, 1), (1, 0, 1), (-1, 0, 1), (0, 1, 1), (0, -1, 1)]
    barrier = pltpu.get_barrier_semaphore()
    for dx, dy, other in around:
        when(
            exists(dx, dy),
            lambda: pl.semaphore_signal(
                barrier, inc=1, device_id=device(dx, dy, other), device_id_type=MESH
            ),
        )

    plus_x = [q for q in range(Q) if velocity[q][0] > 0]
    minus_x = [q for q in range(Q) if velocity[q][0] < 0]
    plus_y = [q for q in range(Q) if velocity[q][1] > 0]
    minus_y = [q for q in range(Q) if velocity[q][1] < 0]

    def clear_x(side):
        plane = 0 if side < 0 else 17
        for q in minus_x if side < 0 else plus_x:
            padded[q, plane, :, :] = jnp.zeros((32, 128), F32)
        for slot in (1, 2):
            beside[slot, plane, :, :] = jnp.zeros((32, 128), F32)
        first = 0 if side < 0 else 24
        for ref in (field, grad):
            ref[first : first + 8, :, :] = jnp.zeros((8, 32, 128), F32)

    def clear_y(side):
        row = 7 if side < 0 else 24
        for q in minus_y if side < 0 else plus_y:
            for i in range(18):
                padded[q, i, row : row + 1, :] = jnp.zeros((1, 128), F32)
        for slot in (3, 4):
            for i in range(18):
                beside[slot, i, row : row + 1, :] = jnp.zeros((1, 128), F32)
        first = 0 if side < 0 else 24
        for ref in (field, grad):
            ref[:, first : first + 8, :] = jnp.zeros((32, 8, 128), F32)

    for side in (-1, 1):
        when(jnp.logical_not(exists(side, 0)), lambda: clear_x(side))
        when(jnp.logical_not(exists(0, side)), lambda: clear_y(side))

    sides_x = jnp.where(low_x, 1, 0) + jnp.where(high_x, 1, 0)
    sides_y = jnp.where(low_y, 1, 0) + jnp.where(high_y, 1, 0)
    pl.semaphore_wait(barrier, 1 + 2 * sides_x + 2 * sides_y + sides_x * sides_y)

    count = [0]

    def remote(src, dst, dx, dy, other, extra=None):
        copy = pltpu.make_async_remote_copy(
            src_ref=src,
            dst_ref=dst,
            send_sem=send_sem.at[count[0]],
            recv_sem=recv_sem.at[count[0]],
            device_id=device(dx, dy, other),
            device_id_type=MESH,
        )
        count[0] += 1
        return (exists(dx, dy), exists(-dx, -dy), copy, extra)

    def both(cond, extra):
        if extra is None:
            return cond
        return extra if cond is True else jnp.logical_and(cond, extra)

    def start(group):
        for sends, _, copy, extra in group:
            when(both(sends, extra and extra[0]), copy.start)

    def arrive(group):
        for _, receives, copy, extra in group:
            when(both(receives, extra and extra[1]), copy.wait_recv)

    def sent(group):
        for sends, _, copy, extra in group:
            when(both(sends, extra and extra[0]), copy.wait_send)

    def slab(ref, dx, dy):
        def own(d):
            return slice(8, 16) if d > 0 else slice(0, 8) if d < 0 else slice(0, 16)

        return ref.at[own(dx), own(dy), :]

    def halo(ref, dx, dy):
        def there(d):
            return slice(0, 8) if d > 0 else slice(24, 32) if d < 0 else slice(8, 24)

        return ref.at[there(dx), there(dy), :]

    order = [(1, 0), (-1, 0), (1, 1), (1, -1), (-1, 1), (-1, -1), (0, 1), (0, -1)]
    design_group = [
        remote(slab(design, dx, dy), halo(field, dx, dy), dx, dy, 0) for dx, dy in order
    ]
    start(design_group)

    faces = []
    for q in range(1, Q):
        cx, cy, cz = velocity[q]

        def pick(c, size):
            return slice(0, 1) if c > 0 else slice(size - 1, size) if c < 0 else slice(0, size)

        def put(c, low, size):
            return (
                slice(low + size, low + size + 1)
                if c > 0
                else slice(low - 1, low) if c < 0 else slice(low, low + size)
            )

        moves = []
        if cx:
            moves.append((cx, 0))
        if cy:
            moves.append((0, cy))
        if cx and cy:
            moves.append((cx, cy))
        for mx, my in moves:
            faces.append(
                remote(
                    adjoint.at[q, pick(mx, 16), pick(my, 16), :],
                    padded.at[q, put(mx, 1, 16), put(my, 8, 16), :],
                    -mx,
                    -my,
                    0,
                )
            )
            if cz:
                mine = Z == (1 if cz > 0 else 0)
                theirs = Z == (0 if cz > 0 else 1)
                faces.append(
                    remote(
                        adjoint.at[q, pick(mx, 16), pick(my, 16), :],
                        beside.at[slot_of[q], put(mx, 1, 16), put(my, 8, 16), :],
                        -mx,
                        -my,
                        1,
                        (mine, theirs),
                    )
                )
    start(faces)
    z_faces = []
    for q in (5, 11, 14, 15, 18):
        z_faces.append(
            remote(
                adjoint.at[q * Z + opposite[q] * (1 - Z)],
                beside.at[slot_of[q], 1:17, 8:24, :],
                0,
                0,
                1,
            )
        )
    start(z_faces)

    loads[1].wait()

    def flow_step(i, carry):
        for half in range(2):
            rows = pl.ds(8 * half, 8)
            f = [flow[q, i, rows, :] for q in range(Q)]
            scale = 1.0 / add_all([(1, f[q]) for q in range(Q)])
            vel = [
                add_all([(velocity[q][a], f[q]) for q in range(Q) if velocity[q][a]]) * scale
                for a in range(3)
            ]
            motion[0, i, rows, :] = scale
            for a in range(3):
                motion[1 + a, i, rows, :] = vel[a]
            motion[4, i, rows, :] = vel[0] * vel[0] + vel[1] * vel[1] + vel[2] * vel[2]
        return carry

    lax.fori_loop(0, 16, flow_step, 0)

    own_taps = tap_matrix(0)
    beside_taps = tap_matrix(jnp.where(Z == 0, 128, -128))

    loads[0].wait()
    arrive(design_group)
    filter_xy(field, middle, smoothed)
    swap = [remote(smoothed, smoothed_beside, 0, 0, 1)]
    start(swap)
    loads[2].wait()
    loads[3].wait()
    own_part = dot(smoothed[...].reshape(256, 128), own_taps)
    arrive(swap)
    filtered = own_part + dot(smoothed_beside[...].reshape(256, 128), beside_taps)
    base = math.tanh(sharpness * threshold)
    denominator = base + math.tanh(sharpness * (1.0 - threshold))
    inner = jnp.tanh(sharpness * (filtered - threshold))
    physical = (base + inner) / denominator
    steep = sharpness * (1.0 - inner * inner) / denominator
    inverse = 1.0 / (ramp_shape + physical)
    damp[...] = (damping_max * ramp_shape * (1.0 - physical) * inverse).reshape(16, 16, 128)
    chain[...] = (
        (-damping_max * ramp_shape * (1.0 + ramp_shape)) * steep * inverse * inverse
    ).reshape(16, 16, 128)

    arrive(faces)
    arrive(z_faces)

    lane = lax.broadcasted_iota(jnp.int32, (8, 128), 1)
    first, last = lane == 0, lane == 127
    first_open = lane == -Z
    last_open = lane == 128 * Z - 1

    def pulled_at(q, i, half):
        cx, cy, cz = velocity[q]
        rows = pl.ds(8 + 8 * half + cy, 8)
        own = padded[q, i + (1 + cx), rows, :]
        if cz == 0:
            return own
        edge = beside[slot_of[q], i + (1 + cx), rows, :]
        if cz > 0:
            joined = jnp.where(first, jnp.where(first_open, edge, 0.0), own)
            return pltpu.roll(joined, 127, 1)
        joined = jnp.where(last, jnp.where(last_open, edge, 0.0), own)
        return pltpu.roll(joined, 1, 1)

    def source_step(i, carry):
        for half in range(2):
            rows = pl.ds(8 * half, 8)
            p = [None] + [pulled_at(q, i, half) for q in range(1, Q)]
            moment = [
                add_all([(velocity[q][a], p[q]) for q in range(1, Q) if velocity[q][a]])
                for a in range(3)
            ]
            vel = [motion[1 + a, i, rows, :] for a in range(3)]
            along = vel[0] * moment[0] + vel[1] * moment[1] + vel[2] * moment[2]
            raw[i, rows, :] = chain[i, rows, :] * (motion[4, i, rows, :] - along)
        return carry

    lax.fori_loop(0, 16, source_step, 0)

    swap_raw = [remote(raw, raw_beside, 0, 0, 1)]
    start(swap_raw)
    own_grad = dot(raw[...].reshape(256, 128), own_taps)
    arrive(swap_raw)
    grad_z = own_grad + dot(raw_beside[...].reshape(256, 128), beside_taps)
    grad[8:24, 8:24, :] = grad_z.reshape(16, 16, 128)

    def own_slab(ref, dx, dy):
        def own(d):
            return slice(16, 24) if d > 0 else slice(8, 16) if d < 0 else slice(8, 24)

        return ref.at[own(dx), own(dy), :]

    grad_group = [
        remote(own_slab(grad, dx, dy), halo(grad, dx, dy), dx, dy, 0) for dx, dy in order
    ]
    start(grad_group)

    def collide_step(i, carry):
        for half in range(2):
            rows = pl.ds(8 * half, 8)
            p = [pulled_at(q, i, half) for q in range(Q)]
            scale = motion[0, i, rows, :]
            vel = [motion[1 + a, i, rows, :] for a in range(3)]
            speed_sq = motion[4, i, rows, :]
            damping = damp[i, rows, :]
            cell = label[i, rows, :]
            wp = [lattice_weight[q] * p[q] for q in range(Q)]
            zeroth = add_all([(1, wp[q]) for q in range(Q)])
            first_m = [
                add_all([(velocity[q][a], wp[q]) for q in range(Q) if velocity[q][a]])
                for a in range(3)
            ]
            second = {}
            for a in range(3):
                for b in range(a, 3):
                    second[a, b] = second[b, a] = add_all(
                        [
                            (velocity[q][a] * velocity[q][b], wp[q])
                            for q in range(Q)
                            if velocity[q][a] * velocity[q][b]
                        ]
                    )
            turned = [
                second[a, 0] * vel[0] + second[a, 1] * vel[1] + second[a, 2] * vel[2]
                for a in range(3)
            ]
            quadric = vel[0] * turned[0] + vel[1] * turned[1] + vel[2] * turned[2]
            eq_scalar = zeroth * (1.0 + 1.5 * speed_sq) - 4.5 * quadric
            eq_vector = [
                3.0 * first_m[a] + 9.0 * turned[a] - 3.0 * zeroth * vel[a] for a in range(3)
            ]
            drag = 2.0 * damping * scale
            fluid, solid, inlet = cell == 0, cell == 1, cell == 2
            for q in range(Q):
                c = velocity[q]
                parts = [(c[a], eq_vector[a]) for a in range(3) if c[a]]
                along_eq = add_all([(1, eq_scalar)] + parts) if parts else eq_scalar
                parts = [(c[a], vel[a]) for a in range(3) if c[a]]
                push = add_all(parts) - speed_sq if parts else -speed_sq
                moved = (1.0 - relax_rate) * p[q] + relax_rate * along_eq + drag * push
                value = jnp.where(
                    fluid,
                    moved,
                    jnp.where(solid, p[opposite[q]], jnp.where(inlet, along_eq, eq_scalar)),
                )
                out[q, i, rows, :] = value
        return carry

    lax.fori_loop(0, 16, collide_step, 0)

    arrive(grad_group)
    for group in (design_group, faces, z_faces, swap, swap_raw, grad_group):
        sent(group)


def final_kernel(next_in, grad, next_out, sensitivity, middle, result, sems):
    whole = pltpu.make_async_copy(next_in, next_out, sems.at[0])
    whole.start()
    filter_xy(grad, middle, result)
    last = pltpu.make_async_copy(result, sensitivity, sems.at[1])
    last.start()
    last.wait()
    whole.wait()


N_COPIES = 64


def local(forward, adjoint, design, mask):
    block = design.shape
    wide = (32, 32, 128)
    anywhere = pl.BlockSpec(memory_space=pl.ANY)
    in_vmem = pl.BlockSpec(memory_space=pltpu.VMEM)
    vmem = lambda shape, dtype=F32: pltpu.VMEM(shape, dtype)
    nxt, grad = pl.pallas_call(
        main_kernel,
        out_shape=(vmem((Q,) + block), vmem(wide)),
        in_specs=[anywhere] * 4,
        out_specs=(in_vmem, in_vmem),
        scratch_shapes=[
            vmem((Q, 18, 32, 128)),
            vmem((5, 18, 32, 128)),
            vmem((Q,) + block),
            vmem(block, jnp.int32),
            vmem(wide),
            vmem((16, 32, 128)),
            vmem(block),
            vmem(block),
            vmem((5,) + block),
            vmem(block),
            vmem(block),
            vmem(block),
            vmem(block),
            pltpu.SemaphoreType.DMA((4,)),
            pltpu.SemaphoreType.DMA((N_COPIES,)),
            pltpu.SemaphoreType.DMA((N_COPIES,)),
        ],
        compiler_params=pltpu.CompilerParams(collective_id=0, has_side_effects=True),
        name="adjoint_main",
    )(forward, adjoint, design, mask)
    keep = lambda a: pltpu.with_memory_space_constraint(a, pltpu.VMEM)
    return pl.pallas_call(
        final_kernel,
        out_shape=(
            jax.ShapeDtypeStruct((Q,) + block, F32),
            jax.ShapeDtypeStruct(block, F32),
        ),
        in_specs=[in_vmem, in_vmem],
        out_specs=(anywhere, anywhere),
        scratch_shapes=[
            vmem((16, 32, 128)),
            vmem(block),
            pltpu.SemaphoreType.DMA((2,)),
        ],
        name="adjoint_final",
    )(keep(nxt), keep(grad))


def solution(mesh):
    return jax.shard_map(
        local,
        mesh=mesh,
        in_specs=(
            P(None, "gx", "gy", "gz"),
            P(None, "gx", "gy", "gz"),
            P("gx", "gy", "gz"),
            P("gx", "gy", "gz"),
        ),
        out_specs=(P(None, "gx", "gy", "gz"), P("gx", "gy", "gz")),
        check_vma=False,
    )
```

time: 125 us -> 33.1 us (0.26)
  the two profiles are of different devices: /device:TPU:109 before, /device:TPU:168 now
where the time goes in v1:
time: 33.1 us; the launch traced here: 33 us
  Pallas kernels  32.3 us (98%)
  between operations  0.64 us (2%)
    pallas_call x1, Pallas kernels, local(): pl.pallas_call(main_kernel, out_shape=(vmem((Q,) + block), vmem(wide)), i...  30.8 us
    pallas_call x1, Pallas kernels, local(): pl.pallas_call(final_kernel, out_shape=(jax.ShapeDtypeStruct((Q,) + block...  1.5 us

profile of v1, /device:TPU:168, one launch (start us, length us, event | category | flops | bytes accessed | tf_op | source)
XLA Modules:
  0.0 33.0 jit_solution(9409465683803575028)
XLA Ops:
  0.6 30.8 %adjoint_main.1 = (f32[19,16,16,128]{3,2,1,0:T(8,128)S(1)}, f32[32,32,128]{2,1,0:T(8,128)S(1)}) custom-call(f32[19,16,16,128]{3,2,1,0:T(8,128)} %forward.1, f32[19,16,16,128]{3,2,1,0:T(8,128)} %adjoint.1, f32[16,16,128]{2,1,0:T(8,128)} %design.1, s32[16,16,128]{2,1,0:T(8,128)} %mask.1), custom_call_target="tpu_custom_call" | custom-call | tf_op jit(solution)/shard_map/adjoint_main/pallas_call | solution.py:487
  31.5 1.5 %adjoint_final.1 = (f32[19,16,16,128]{3,2,1,0:T(8,128)}, f32[16,16,128]{2,1,0:T(8,128)}) custom-call(f32[19,16,16,128]{3,2,1,0:T(8,128)S(1)} %get-tuple-element.4.next_in, f32[32,32,128]{2,1,0:T(8,128)S(1)} %get-tuple-element.5.grad), custom_call_target="tpu_custom_call" | custom-call | tf_op jit(solution)/shard_map/adjoint_final/pallas_call | solution.py:514

commit v2 on v1

--- a/solution.py
+++ b/solution.py
@@ -110,6 +110,10 @@
     grad,
     padded,
     beside,
+    face_x,
+    face_y,
+    halo_x,
+    halo_y,
     flow,
     label,
     field,
@@ -158,7 +162,7 @@
         load.start()
 
     around = [(dx, dy, 0) for dx in (-1, 0, 1) for dy in (-1, 0, 1) if dx or dy]
-    around += [(0, 0, 1), (1, 0, 1), (-1, 0, 1), (0, 1, 1), (0, -1, 1)]
+    around.append((0, 0, 1))
     barrier = pltpu.get_barrier_semaphore()
     for dx, dy, other in around:
         when(
@@ -177,8 +181,6 @@
         plane = 0 if side < 0 else 17
         for q in minus_x if side < 0 else plus_x:
             padded[q, plane, :, :] = jnp.zeros((32, 128), F32)
-        for slot in (1, 2):
-            beside[slot, plane, :, :] = jnp.zeros((32, 128), F32)
         first = 0 if side < 0 else 24
         for ref in (field, grad):
             ref[first : first + 8, :, :] = jnp.zeros((8, 32, 128), F32)
@@ -188,9 +190,6 @@
         for q in minus_y if side < 0 else plus_y:
             for i in range(18):
                 padded[q, i, row : row + 1, :] = jnp.zeros((1, 128), F32)
-        for slot in (3, 4):
-            for i in range(18):
-                beside[slot, i, row : row + 1, :] = jnp.zeros((1, 128), F32)
         first = 0 if side < 0 else 24
         for ref in (field, grad):
             ref[:, first : first + 8, :] = jnp.zeros((32, 8, 128), F32)
@@ -201,7 +200,7 @@
 
     sides_x = jnp.where(low_x, 1, 0) + jnp.where(high_x, 1, 0)
     sides_y = jnp.where(low_y, 1, 0) + jnp.where(high_y, 1, 0)
-    pl.semaphore_wait(barrier, 1 + 2 * sides_x + 2 * sides_y + sides_x * sides_y)
+    pl.semaphore_wait(barrier, 1 + sides_x + sides_y + sides_x * sides_y)
 
     count = [0]
 
@@ -252,62 +251,10 @@
     ]
     start(design_group)
 
-    faces = []
-    for q in range(1, Q):
-        cx, cy, cz = velocity[q]
-
-        def pick(c, size):
-            return slice(0, 1) if c > 0 else slice(size - 1, size) if c < 0 else slice(0, size)
-
-        def put(c, low, size):
-            return (
-                slice(low + size, low + size + 1)
-                if c > 0
-                else slice(low - 1, low) if c < 0 else slice(low, low + size)
-            )
-
-        moves = []
-        if cx:
-            moves.append((cx, 0))
-        if cy:
-            moves.append((0, cy))
-        if cx and cy:
-            moves.append((cx, cy))
-        for mx, my in moves:
-            faces.append(
-                remote(
-                    adjoint.at[q, pick(mx, 16), pick(my, 16), :],
-                    padded.at[q, put(mx, 1, 16), put(my, 8, 16), :],
-                    -mx,
-                    -my,
-                    0,
-                )
-            )
-            if cz:
-                mine = Z == (1 if cz > 0 else 0)
-                theirs = Z == (0 if cz > 0 else 1)
-                faces.append(
-                    remote(
-                        adjoint.at[q, pick(mx, 16), pick(my, 16), :],
-                        beside.at[slot_of[q], put(mx, 1, 16), put(my, 8, 16), :],
-                        -mx,
-                        -my,
-                        1,
-                        (mine, theirs),
-                    )
-                )
-    start(faces)
-    z_faces = []
-    for q in (5, 11, 14, 15, 18):
-        z_faces.append(
-            remote(
-                adjoint.at[q * Z + opposite[q] * (1 - Z)],
-                beside.at[slot_of[q], 1:17, 8:24, :],
-                0,
-                0,
-                1,
-            )
-        )
+    z_faces = [
+        remote(adjoint.at[q * Z + opposite[q] * (1 - Z)], beside.at[slot_of[q]], 0, 0, 1)
+        for q in (5, 11, 14, 15, 18)
+    ]
     start(z_faces)
 
     loads[1].wait()
@@ -332,12 +279,56 @@
     own_taps = tap_matrix(0)
     beside_taps = tap_matrix(jnp.where(Z == 0, 128, -128))
 
+    lane = lax.broadcasted_iota(jnp.int32, (16, 128), 1)
+    first, last = lane == 0, lane == 127
+    first_open = lane == -Z
+    last_open = lane == 128 * Z - 1
+    loads[2].wait()
+    arrive(z_faces)
+
+    def pull_z(i, carry):
+        for q in slot_of:
+            own = padded[q, i + 1, 8:24, :]
+            edge = beside[slot_of[q], i, :, :]
+            if velocity[q][2] > 0:
+                joined = jnp.where(first, jnp.where(first_open, edge, 0.0), own)
+                shifted = pltpu.roll(joined, 127, 1)
+            else:
+                joined = jnp.where(last, jnp.where(last_open, edge, 0.0), own)
+                shifted = pltpu.roll(joined, 1, 1)
+            padded[q, i + 1, 8:24, :] = shifted
+        return carry
+
+    lax.fori_loop(0, 16, pull_z, 0)
+    for k in range(5):
+        face_x[0, k, :, :] = padded[minus_x[k], 16, 8:24, :]
+        face_x[1, k, :, :] = padded[plus_x[k], 1, 8:24, :]
+        face_y[0, k, :, :] = padded[minus_y[k], 1:17, 23, :]
+        face_y[1, k, :, :] = padded[plus_y[k], 1:17, 8, :]
+    faces = [
+        remote(face_x.at[0], halo_x.at[0], 1, 0, 0),
+        remote(face_x.at[1], halo_x.at[1], -1, 0, 0),
+        remote(face_y.at[0], halo_y.at[0], 0, 1, 0),
+        remote(face_y.at[1], halo_y.at[1], 0, -1, 0),
+    ]
+    for q in (7, 8, 9, 10):
+        cx, cy, cz = velocity[q]
+        faces.append(
+            remote(
+                adjoint.at[q, slice(0, 1) if cx > 0 else slice(15, 16), slice(0, 1) if cy > 0 else slice(15, 16), :],
+                padded.at[q, slice(17, 18) if cx > 0 else slice(0, 1), slice(24, 25) if cy > 0 else slice(7, 8), :],
+                -cx,
+                -cy,
+                0,
+            )
+        )
+    start(faces)
+
     loads[0].wait()
     arrive(design_group)
     filter_xy(field, middle, smoothed)
     swap = [remote(smoothed, smoothed_beside, 0, 0, 1)]
     start(swap)
-    loads[2].wait()
     loads[3].wait()
     own_part = dot(smoothed[...].reshape(256, 128), own_taps)
     arrive(swap)
@@ -354,25 +345,24 @@
     ).reshape(16, 16, 128)
 
     arrive(faces)
-    arrive(z_faces)
-
-    lane = lax.broadcasted_iota(jnp.int32, (8, 128), 1)
-    first, last = lane == 0, lane == 127
-    first_open = lane == -Z
-    last_open = lane == 128 * Z - 1
+
+    def place_x(side):
+        for k in range(5):
+            q, plane = ((plus_x if side else minus_x)[k], 17 if side else 0)
+            padded[q, plane, 8:24, :] = halo_x[side, k, :, :]
+
+    def place_y(side):
+        for k in range(5):
+            q, row = ((plus_y if side else minus_y)[k], 24 if side else 7)
+            padded[q, 1:17, row, :] = halo_y[side, k, :, :]
+
+    for side in (0, 1):
+        when(exists(2 * side - 1, 0), lambda: place_x(side))
+        when(exists(0, 2 * side - 1), lambda: place_y(side))
 
     def pulled_at(q, i, half):
         cx, cy, cz = velocity[q]
-        rows = pl.ds(8 + 8 * half + cy, 8)
-        own = padded[q, i + (1 + cx), rows, :]
-        if cz == 0:
-            return own
-        edge = beside[slot_of[q], i + (1 + cx), rows, :]
-        if cz > 0:
-            joined = jnp.where(first, jnp.where(first_open, edge, 0.0), own)
-            return pltpu.roll(joined, 127, 1)
-        joined = jnp.where(last, jnp.where(last_open, edge, 0.0), own)
-        return pltpu.roll(joined, 1, 1)
+        return padded[q, i + (1 + cx), pl.ds(8 + 8 * half + cy, 8), :]
 
     def source_step(i, carry):
         for half in range(2):
@@ -491,7 +481,11 @@
         out_specs=(in_vmem, in_vmem),
         scratch_shapes=[
             vmem((Q, 18, 32, 128)),
-            vmem((5, 18, 32, 128)),
+            vmem((5,) + block),
+            vmem((2, 5, 16, 128)),
+            vmem((2, 5, 16, 128)),
+            vmem((2, 5, 16, 128)),
+            vmem((2, 5, 16, 128)),
             vmem((Q,) + block),
             vmem(block, jnp.int32),
             vmem(wide),

time: 33.1 us -> 30.4 us (0.918)
  Pallas kernels: 32.3 us -> 29.7 us
    pallas_call x1, Pallas kernels: 30.8 us -> 28.2 us  [local(): pl.pallas_call(main_kernel, out_shape=(vmem((Q,) + block), vmem(wide)), i...]
where the time goes in v2:
time: 30.4 us; the launch traced here: 30.3 us
  Pallas kernels  29.7 us (98%)
  between operations  0.64 us (2%)
    pallas_call x1, Pallas kernels, local(): pl.pallas_call(main_kernel, out_shape=(vmem((Q,) + block), vmem(wide)), i...  28.2 us
    pallas_call x1, Pallas kernels, local(): pl.pallas_call(final_kernel, out_shape=(jax.ShapeDtypeStruct((Q,) + block...  1.5 us

profile of v2, /device:TPU:168, one launch (start us, length us, event | category | flops | bytes accessed | tf_op | source)
XLA Modules:
  0.0 30.3 jit_solution(7020057910565936653)
XLA Ops:
  0.6 28.2 %adjoint_main.1 = (f32[19,16,16,128]{3,2,1,0:T(8,128)S(1)}, f32[32,32,128]{2,1,0:T(8,128)S(1)}) custom-call(f32[19,16,16,128]{3,2,1,0:T(8,128)} %forward.1, f32[19,16,16,128]{3,2,1,0:T(8,128)} %adjoint.1, f32[16,16,128]{2,1,0:T(8,128)} %design.1, s32[16,16,128]{2,1,0:T(8,128)} %mask.1), custom_call_target="tpu_custom_call" | custom-call | tf_op jit(solution)/shard_map/adjoint_main/pallas_call | solution.py:477
  28.8 1.5 %adjoint_final.1 = (f32[19,16,16,128]{3,2,1,0:T(8,128)}, f32[16,16,128]{2,1,0:T(8,128)}) custom-call(f32[19,16,16,128]{3,2,1,0:T(8,128)S(1)} %get-tuple-element.4.next_in, f32[32,32,128]{2,1,0:T(8,128)S(1)} %get-tuple-element.5.grad), custom_call_target="tpu_custom_call" | custom-call | tf_op jit(solution)/shard_map/adjoint_final/pallas_call | solution.py:508

commit v3 on v2

--- a/solution.py
+++ b/solution.py
@@ -66,25 +66,55 @@
     return total
 
 
-def filter_xy(source, middle, result):
-    def along_x(group, carry):
-        rows = pl.ds(pl.multiple_of(group * 8, 8), 8)
-        planes = [source[i, rows, :] for i in range(32)]
+def filter_xy(source, edges, middle, result):
+    Z = lax.axis_index("gz")
+    lane = lax.broadcasted_iota(jnp.int32, (8, 128), 1)
+    lowest = 120 * (1 - Z)
+    edge = jnp.logical_and(lane >= lowest, lane < lowest + 8)
+
+    def spread(n, u):
+        whole_row = edges[n, :, :]
+        if u:
+            whole_row = pltpu.roll(whole_row, 128 - 8 * u, 1)
+        return jnp.where(edge, whole_row, 0.0)
+
+    for group in range(4):
+        rows = slice(8 * group, 8 * group + 8)
+        dy = 1 if group == 0 else -1 if group == 3 else 0
+        planes = []
+        for i in range(32):
+            plane = source[i, rows, :]
+            dx = 1 if i < 8 else -1 if i >= 24 else 0
+            if dx or dy:
+                if dx == 0:
+                    u = i - 8
+                else:
+                    u = 2 * (i % 8) + (group - 1 if dy == 0 else 1 if dy > 0 else 0)
+                plane = plane + spread(ORDER.index((dx, dy)), u)
+            planes.append(plane)
         for i in range(16):
             middle[i, rows, :] = symmetric(lambda k: planes[i + 8 + k])
+    filter_y(middle, result)
+
+
+def filter_y(middle, result):
+    def along_y(i, carry):
+        rows = [middle[i, pl.ds(at, 8), :] for at in range(25)]
+        for half in range(2):
+            result[i, pl.ds(8 * half, 8), :] = symmetric(lambda k: rows[8 + 8 * half + k])
         return carry
 
-    lax.fori_loop(0, 4, along_x, 0)
-
-    def along_y(i, carry):
-        for half in range(2):
-            at = 8 + 8 * half
-            result[i, pl.ds(8 * half, 8), :] = symmetric(
-                lambda k: middle[i, pl.ds(at + k, 8), :]
-            )
-        return carry
-
     lax.fori_loop(0, 16, along_y, 0)
+
+
+ORDER = [(1, 0), (-1, 0), (1, 1), (1, -1), (-1, 1), (-1, -1), (0, 1), (0, -1)]
+
+
+def packed(units):
+    total = units[0]
+    for u in range(1, 16):
+        total = total + pltpu.roll(units[u], 8 * u, 1)
+    return total
 
 
 def dot(a, b):
@@ -108,6 +138,7 @@
     mask,
     out,
     grad,
+    edges,
     padded,
     beside,
     face_x,
@@ -116,15 +147,22 @@
     halo_y,
     flow,
     label,
+    plain,
+    own_design,
+    design_beside,
     field,
+    field_out,
+    field_edges,
     middle,
     smoothed,
-    smoothed_beside,
     motion,
     chain,
     damp,
     raw,
     raw_beside,
+    lean,
+    own_side,
+    edge_out,
     local_sem,
     send_sem,
     recv_sem,
@@ -153,7 +191,7 @@
         return (X + dx, Y + dy, 1 - Z if other else Z)
 
     loads = [
-        pltpu.make_async_copy(design, field.at[8:24, 8:24, :], local_sem.at[0]),
+        pltpu.make_async_copy(design, plain, local_sem.at[0]),
         pltpu.make_async_copy(forward, flow, local_sem.at[1]),
         pltpu.make_async_copy(adjoint, padded.at[:, 1:17, 8:24, :], local_sem.at[2]),
         pltpu.make_async_copy(mask, label, local_sem.at[3]),
@@ -177,27 +215,53 @@
     plus_y = [q for q in range(Q) if velocity[q][1] > 0]
     minus_y = [q for q in range(Q) if velocity[q][1] < 0]
 
+    for q in minus_x + plus_x:
+        padded[q, 17 if q in plus_x else 0, :, :] = jnp.zeros((32, 128), F32)
+    for q in minus_y + plus_y:
+        padded[q, 1:17, 24 if q in plus_y else 7, :] = jnp.zeros((16, 128), F32)
+    for side in range(2):
+        for k in range(5):
+            for row in (7, 24):
+                halo_y[side, k, row : row + 1, :] = jnp.zeros((1, 128), F32)
+
     def clear_x(side):
-        plane = 0 if side < 0 else 17
-        for q in minus_x if side < 0 else plus_x:
-            padded[q, plane, :, :] = jnp.zeros((32, 128), F32)
-        first = 0 if side < 0 else 24
+        halo_x[max(side, 0), :, 8:24, :] = jnp.zeros((5, 16, 128), F32)
+        begin = 0 if side < 0 else 24
         for ref in (field, grad):
-            ref[first : first + 8, :, :] = jnp.zeros((8, 32, 128), F32)
+            ref[begin : begin + 8, :, :] = jnp.zeros((8, 32, 128), F32)
 
     def clear_y(side):
-        row = 7 if side < 0 else 24
-        for q in minus_y if side < 0 else plus_y:
-            for i in range(18):
-                padded[q, i, row : row + 1, :] = jnp.zeros((1, 128), F32)
-        first = 0 if side < 0 else 24
+        halo_y[max(side, 0), :, 8:24, :] = jnp.zeros((5, 16, 128), F32)
+        begin = 0 if side < 0 else 24
         for ref in (field, grad):
-            ref[:, first : first + 8, :] = jnp.zeros((32, 8, 128), F32)
-
+            ref[:, begin : begin + 8, :] = jnp.zeros((32, 8, 128), F32)
+
+    def corner(q):
+        cx, cy, cz = velocity[q]
+        k = (plus_x if cx > 0 else minus_x).index(q)
+        return (1 if cx > 0 else 0), k, slice(24, 25) if cy > 0 else slice(7, 8)
+
+    def clear_corner(q):
+        side, k, row = corner(q)
+        halo_x[side, k, row, :] = jnp.zeros((1, 128), F32)
+
+    def clear_edge(n):
+        for ref in (edges, field_edges):
+            ref[n, :, :] = jnp.zeros((8, 128), F32)
+
+    for n, (dx, dy) in enumerate(ORDER):
+        when(jnp.logical_not(exists(-dx, -dy)), lambda: clear_edge(n))
+    for q in (7, 8, 9, 10):
+        cx, cy, cz = velocity[q]
+        when(jnp.logical_not(exists(cx, cy)), lambda: clear_corner(q))
     for side in (-1, 1):
         when(jnp.logical_not(exists(side, 0)), lambda: clear_x(side))
         when(jnp.logical_not(exists(0, side)), lambda: clear_y(side))
 
+    own_taps = tap_matrix(0)
+    beside_taps = tap_matrix(jnp.where(Z == 0, 128, -128))
+    loads[0].wait()
+    own_design[...] = dot(plain[...].reshape(256, 128), own_taps).reshape(16, 16, 128)
     sides_x = jnp.where(low_x, 1, 0) + jnp.where(high_x, 1, 0)
     sides_y = jnp.where(low_y, 1, 0) + jnp.where(high_y, 1, 0)
     pl.semaphore_wait(barrier, 1 + sides_x + sides_y + sides_x * sides_y)
@@ -245,10 +309,32 @@
 
         return ref.at[there(dx), there(dy), :]
 
-    order = [(1, 0), (-1, 0), (1, 1), (1, -1), (-1, 1), (-1, -1), (0, 1), (0, -1)]
-    design_group = [
-        remote(slab(design, dx, dy), halo(field, dx, dy), dx, dy, 0) for dx, dy in order
-    ]
+    def slabs(own, result):
+        return [remote(slab(own, dx, dy), halo(result, dx, dy), dx, dy, 0) for dx, dy in ORDER]
+
+    def join(own, received, result, packs, landing):
+        other = dot(received[...].reshape(256, 128), beside_taps).reshape(16, 16, 128)
+        result[8:24, 8:24, :] = own[...] + other
+        for side in range(2):
+            at = 0 if side else 8
+            packs[side, :, :] = packed(
+                [other[at + p, 8 * g : 8 * g + 8, :] for p in range(8) for g in range(2)]
+            )
+            packs[2 + side, :, :] = packed([other[i, at : at + 8, :] for i in range(16)])
+        return [
+            remote(
+                packs.at[(0 if dx > 0 else 1) if dx else (2 if dy > 0 else 3)],
+                landing.at[n],
+                dx,
+                dy,
+                0,
+            )
+            for n, (dx, dy) in enumerate(ORDER)
+        ]
+
+    swap = [remote(design, design_beside, 0, 0, 1)]
+    design_group = slabs(own_design, field)
+    start(swap)
     start(design_group)
 
     z_faces = [
@@ -256,6 +342,56 @@
         for q in (5, 11, 14, 15, 18)
     ]
     start(z_faces)
+
+    arrive(swap)
+    field_group = join(own_design, design_beside, field, field_out, field_edges)
+    start(field_group)
+
+    lane = lax.broadcasted_iota(jnp.int32, (16, 128), 1)
+    first, last = lane == 0, lane == 127
+    first_open = lane == -Z
+    last_open = lane == 128 * Z - 1
+    loads[2].wait()
+    arrive(z_faces)
+
+    def pull_z(i, carry):
+        for q in slot_of:
+            own = padded[q, i + 1, 8:24, :]
+            edge = beside[slot_of[q], i, :, :]
+            if velocity[q][2] > 0:
+                joined = jnp.where(first, jnp.where(first_open, edge, 0.0), own)
+                shifted = pltpu.roll(joined, 127, 1)
+            else:
+                joined = jnp.where(last, jnp.where(last_open, edge, 0.0), own)
+                shifted = pltpu.roll(joined, 1, 1)
+            padded[q, i + 1, 8:24, :] = shifted
+        return carry
+
+    lax.fori_loop(0, 16, pull_z, 0)
+    for k in range(5):
+        face_x[0, k, :, :] = padded[minus_x[k], 16, 8:24, :]
+        face_x[1, k, :, :] = padded[plus_x[k], 1, 8:24, :]
+        face_y[0, k, :, :] = padded[minus_y[k], 1:17, 23, :]
+        face_y[1, k, :, :] = padded[plus_y[k], 1:17, 8, :]
+    faces = [
+        remote(face_x.at[0], halo_x.at[0, :, 8:24, :], 1, 0, 0),
+        remote(face_x.at[1], halo_x.at[1, :, 8:24, :], -1, 0, 0),
+        remote(face_y.at[0], halo_y.at[0, :, 8:24, :], 0, 1, 0),
+        remote(face_y.at[1], halo_y.at[1, :, 8:24, :], 0, -1, 0),
+    ]
+    for q in (7, 8, 9, 10):
+        cx, cy, cz = velocity[q]
+        side, k, row = corner(q)
+        faces.append(
+            remote(
+                adjoint.at[q, 0 if cx > 0 else 15, slice(0, 1) if cy > 0 else slice(15, 16), :],
+                halo_x.at[side, k, row, :],
+                -cx,
+                -cy,
+                0,
+            )
+        )
+    start(faces)
 
     loads[1].wait()
 
@@ -276,63 +412,28 @@
 
     lax.fori_loop(0, 16, flow_step, 0)
 
-    own_taps = tap_matrix(0)
-    beside_taps = tap_matrix(jnp.where(Z == 0, 128, -128))
-
-    lane = lax.broadcasted_iota(jnp.int32, (16, 128), 1)
-    first, last = lane == 0, lane == 127
-    first_open = lane == -Z
-    last_open = lane == 128 * Z - 1
-    loads[2].wait()
-    arrive(z_faces)
-
-    def pull_z(i, carry):
-        for q in slot_of:
-            own = padded[q, i + 1, 8:24, :]
-            edge = beside[slot_of[q], i, :, :]
-            if velocity[q][2] > 0:
-                joined = jnp.where(first, jnp.where(first_open, edge, 0.0), own)
-                shifted = pltpu.roll(joined, 127, 1)
-            else:
-                joined = jnp.where(last, jnp.where(last_open, edge, 0.0), own)
-                shifted = pltpu.roll(joined, 1, 1)
-            padded[q, i + 1, 8:24, :] = shifted
+
+    def pulled_at(q, i, half):
+        cx, cy, cz = velocity[q]
+        return padded[q, i + (1 + cx), pl.ds(8 + 8 * half + cy, 8), :]
+
+    def moment_step(i, carry):
+        for half in range(2):
+            rows = pl.ds(8 * half, 8)
+            p = [None] + [pulled_at(q, i, half) for q in range(1, Q)]
+            total = motion[4, i, rows, :]
+            for axis in range(3):
+                moment = add_all([(velocity[q][axis], p[q]) for q in range(1, Q) if velocity[q][axis]])
+                total = total - motion[1 + axis, i, rows, :] * moment
+            lean[i, rows, :] = total
         return carry
 
-    lax.fori_loop(0, 16, pull_z, 0)
-    for k in range(5):
-        face_x[0, k, :, :] = padded[minus_x[k], 16, 8:24, :]
-        face_x[1, k, :, :] = padded[plus_x[k], 1, 8:24, :]
-        face_y[0, k, :, :] = padded[minus_y[k], 1:17, 23, :]
-        face_y[1, k, :, :] = padded[plus_y[k], 1:17, 8, :]
-    faces = [
-        remote(face_x.at[0], halo_x.at[0], 1, 0, 0),
-        remote(face_x.at[1], halo_x.at[1], -1, 0, 0),
-        remote(face_y.at[0], halo_y.at[0], 0, 1, 0),
-        remote(face_y.at[1], halo_y.at[1], 0, -1, 0),
-    ]
-    for q in (7, 8, 9, 10):
-        cx, cy, cz = velocity[q]
-        faces.append(
-            remote(
-                adjoint.at[q, slice(0, 1) if cx > 0 else slice(15, 16), slice(0, 1) if cy > 0 else slice(15, 16), :],
-                padded.at[q, slice(17, 18) if cx > 0 else slice(0, 1), slice(24, 25) if cy > 0 else slice(7, 8), :],
-                -cx,
-                -cy,
-                0,
-            )
-        )
-    start(faces)
-
-    loads[0].wait()
+    lax.fori_loop(0, 16, moment_step, 0)
     arrive(design_group)
-    filter_xy(field, middle, smoothed)
-    swap = [remote(smoothed, smoothed_beside, 0, 0, 1)]
-    start(swap)
+    arrive(field_group)
+    filter_xy(field, field_edges, middle, smoothed)
     loads[3].wait()
-    own_part = dot(smoothed[...].reshape(256, 128), own_taps)
-    arrive(swap)
-    filtered = own_part + dot(smoothed_beside[...].reshape(256, 128), beside_taps)
+    filtered = smoothed[...].reshape(256, 128)
     base = math.tanh(sharpness * threshold)
     denominator = base + math.tanh(sharpness * (1.0 - threshold))
     inner = jnp.tanh(sharpness * (filtered - threshold))
@@ -344,58 +445,57 @@
         (-damping_max * ramp_shape * (1.0 + ramp_shape)) * steep * inverse * inverse
     ).reshape(16, 16, 128)
 
+    source_own = chain[...] * lean[...]
+    raw[...] = source_own
+    own_side[...] = dot(source_own.reshape(256, 128), own_taps).reshape(16, 16, 128)
     arrive(faces)
 
-    def place_x(side):
-        for k in range(5):
-            q, plane = ((plus_x if side else minus_x)[k], 17 if side else 0)
-            padded[q, plane, 8:24, :] = halo_x[side, k, :, :]
-
-    def place_y(side):
-        for k in range(5):
-            q, row = ((plus_y if side else minus_y)[k], 24 if side else 7)
-            padded[q, 1:17, row, :] = halo_y[side, k, :, :]
-
-    for side in (0, 1):
-        when(exists(2 * side - 1, 0), lambda: place_x(side))
-        when(exists(0, 2 * side - 1), lambda: place_y(side))
-
-    def pulled_at(q, i, half):
-        cx, cy, cz = velocity[q]
-        return padded[q, i + (1 + cx), pl.ds(8 + 8 * half + cy, 8), :]
-
-    def source_step(i, carry):
-        for half in range(2):
-            rows = pl.ds(8 * half, 8)
-            p = [None] + [pulled_at(q, i, half) for q in range(1, Q)]
-            moment = [
-                add_all([(velocity[q][a], p[q]) for q in range(1, Q) if velocity[q][a]])
-                for a in range(3)
-            ]
-            vel = [motion[1 + a, i, rows, :] for a in range(3)]
-            along = vel[0] * moment[0] + vel[1] * moment[1] + vel[2] * moment[2]
-            raw[i, rows, :] = chain[i, rows, :] * (motion[4, i, rows, :] - along)
-        return carry
-
-    lax.fori_loop(0, 16, source_step, 0)
-
+    changes = []
+    for side in range(2):
+        members = plus_x if side else minus_x
+        i = 15 if side else 0
+        come = [halo_x[side, k, 8 + velocity[q][1] : 24 + velocity[q][1], :] for k, q in enumerate(members)]
+        change = None
+        for axis in range(3):
+            part = add_all([(velocity[q][axis], come[k]) for k, q in enumerate(members) if velocity[q][axis]])
+            part = motion[1 + axis, i, :, :] * part
+            change = part if change is None else change + part
+        change = -chain[i, :, :] * change
+        raw[i, :, :] = raw[i, :, :] + change
+        changes.append(change)
+    for side in range(2):
+        members = plus_y if side else minus_y
+        row = 15 if side else 0
+        come = [halo_y[side, k, 8 + velocity[q][0] : 24 + velocity[q][0], :] for k, q in enumerate(members)]
+        change = None
+        for axis in range(3):
+            part = add_all([(velocity[q][axis], come[k]) for k, q in enumerate(members) if velocity[q][axis]])
+            part = motion[1 + axis, :, row, :] * part
+            change = part if change is None else change + part
+        change = -chain[:, row, :] * change
+        raw[:, row, :] = raw[:, row, :] + change
+        changes.append(change)
     swap_raw = [remote(raw, raw_beside, 0, 0, 1)]
     start(swap_raw)
-    own_grad = dot(raw[...].reshape(256, 128), own_taps)
+    turned = dot(jnp.concatenate(changes, axis=0), own_taps)
+    own_side[0, :, :] = own_side[0, :, :] + turned[0:16]
+    own_side[15, :, :] = own_side[15, :, :] + turned[16:32]
+    own_side[:, 0, :] = own_side[:, 0, :] + turned[32:48]
+    own_side[:, 15, :] = own_side[:, 15, :] + turned[48:64]
+    grad_group = slabs(own_side, grad)
+    start(grad_group)
     arrive(swap_raw)
-    grad_z = own_grad + dot(raw_beside[...].reshape(256, 128), beside_taps)
-    grad[8:24, 8:24, :] = grad_z.reshape(16, 16, 128)
-
-    def own_slab(ref, dx, dy):
-        def own(d):
-            return slice(16, 24) if d > 0 else slice(8, 16) if d < 0 else slice(8, 24)
-
-        return ref.at[own(dx), own(dy), :]
-
-    grad_group = [
-        remote(own_slab(grad, dx, dy), halo(grad, dx, dy), dx, dy, 0) for dx, dy in order
-    ]
-    start(grad_group)
+    edge_group = join(own_side, raw_beside, grad, edge_out, edges)
+    start(edge_group)
+    for side in range(2):
+        for k in range(5):
+            q = (plus_x if side else minus_x)[k]
+            padded[q, 17 if side else 0, 8:24, :] = halo_x[side, k, 8:24, :]
+            q = (plus_y if side else minus_y)[k]
+            padded[q, 1:17, 24 if side else 7, :] = halo_y[side, k, 8:24, :]
+    for q in (7, 8, 9, 10):
+        side, k, row = corner(q)
+        padded[q, 17 if side else 0, row, :] = halo_x[side, k, row, :]
 
     def collide_step(i, carry):
         for half in range(2):
@@ -451,14 +551,15 @@
     lax.fori_loop(0, 16, collide_step, 0)
 
     arrive(grad_group)
-    for group in (design_group, faces, z_faces, swap, swap_raw, grad_group):
+    arrive(edge_group)
+    for group in (design_group, faces, z_faces, swap, field_group, swap_raw, grad_group, edge_group):
         sent(group)
 
 
-def final_kernel(next_in, grad, next_out, sensitivity, middle, result, sems):
+def final_kernel(next_in, grad, edges, next_out, sensitivity, middle, result, sems):
     whole = pltpu.make_async_copy(next_in, next_out, sems.at[0])
     whole.start()
-    filter_xy(grad, middle, result)
+    filter_xy(grad, edges, middle, result)
     last = pltpu.make_async_copy(result, sensitivity, sems.at[1])
     last.start()
     last.wait()
@@ -474,29 +575,36 @@
     anywhere = pl.BlockSpec(memory_space=pl.ANY)
     in_vmem = pl.BlockSpec(memory_space=pltpu.VMEM)
     vmem = lambda shape, dtype=F32: pltpu.VMEM(shape, dtype)
-    nxt, grad = pl.pallas_call(
+    nxt, grad, edges = pl.pallas_call(
         main_kernel,
-        out_shape=(vmem((Q,) + block), vmem(wide)),
+        out_shape=(vmem((Q,) + block), vmem(wide), vmem((8, 8, 128))),
         in_specs=[anywhere] * 4,
-        out_specs=(in_vmem, in_vmem),
+        out_specs=(in_vmem,) * 3,
         scratch_shapes=[
             vmem((Q, 18, 32, 128)),
             vmem((5,) + block),
             vmem((2, 5, 16, 128)),
             vmem((2, 5, 16, 128)),
-            vmem((2, 5, 16, 128)),
-            vmem((2, 5, 16, 128)),
+            vmem((2, 5, 32, 128)),
+            vmem((2, 5, 32, 128)),
             vmem((Q,) + block),
             vmem(block, jnp.int32),
+            vmem(block),
+            vmem(block),
+            vmem(block),
             vmem(wide),
+            vmem((4, 8, 128)),
+            vmem((8, 8, 128)),
             vmem((16, 32, 128)),
             vmem(block),
-            vmem(block),
             vmem((5,) + block),
             vmem(block),
             vmem(block),
             vmem(block),
             vmem(block),
+            vmem(block),
+            vmem(block),
+            vmem((4, 8, 128)),
             pltpu.SemaphoreType.DMA((4,)),
             pltpu.SemaphoreType.DMA((N_COPIES,)),
             pltpu.SemaphoreType.DMA((N_COPIES,)),
@@ -511,7 +619,7 @@
             jax.ShapeDtypeStruct((Q,) + block, F32),
             jax.ShapeDtypeStruct(block, F32),
         ),
-        in_specs=[in_vmem, in_vmem],
+        in_specs=[in_vmem] * 3,
         out_specs=(anywhere, anywhere),
         scratch_shapes=[
             vmem((16, 32, 128)),
@@ -519,7 +627,7 @@
             pltpu.SemaphoreType.DMA((2,)),
         ],
         name="adjoint_final",
-    )(keep(nxt), keep(grad))
+    )(keep(nxt), keep(grad), keep(edges))
 
 
 def solution(mesh):

time: 30.4 us -> 28.2 us (0.928)
  Pallas kernels: 29.7 us -> 27.5 us
    pallas_call x1, Pallas kernels: 28.2 us -> 25.9 us  [local(): pl.pallas_call(main_kernel, out_shape=(vmem((Q,) + block), vmem(wide), vm...]
where the time goes in v3:
time: 28.2 us; the launch traced here: 28.1 us
  Pallas kernels  27.5 us (98%)
  between operations  0.64 us (2%)
    pallas_call x1, Pallas kernels, local(): pl.pallas_call(main_kernel, out_shape=(vmem((Q,) + block), vmem(wide), vm...  25.9 us
    pallas_call x1, Pallas kernels, local(): pl.pallas_call(final_kernel, out_shape=(jax.ShapeDtypeStruct((Q,) + block...  1.58 us

profile of v3, /device:TPU:168, one launch (start us, length us, event | category | flops | bytes accessed | tf_op | source)
XLA Modules:
  0.0 28.1 jit_solution(6297476249938933457)
XLA Ops:
  0.6 25.9 %adjoint_main.1 = (f32[19,16,16,128]{3,2,1,0:T(8,128)S(1)}, f32[32,32,128]{2,1,0:T(8,128)S(1)}, f32[8,8,128]{2,1,0:T(8,128)S(1)}) custom-call(f32[19,16,16,128]{3,2,1,0:T(8,128)} %forward.1, f32[19,16,16,128]{3,2,1,0:T(8,128)} %adjoint.1, f32[16,16,128]{2,1,0:T(8,128)} %design.1, s32[16,16,128]{2,1,0:T(8,128)} %mask.1), custom_call_target="tpu_custom_call" | custom-call | tf_op jit(solution)/shard_map/adjoint_main/pallas_call | solution.py:578
  26.5 1.6 %adjoint_final.1 = (f32[19,16,16,128]{3,2,1,0:T(8,128)}, f32[16,16,128]{2,1,0:T(8,128)}) custom-call(f32[19,16,16,128]{3,2,1,0:T(8,128)S(1)} %get-tuple-element.5.next_in, f32[32,32,128]{2,1,0:T(8,128)S(1)} %get-tuple-element.6.grad, f32[8,8,128]{2,1,0:T(8,128)S(1)} %get-tuple-element.7.edges), custom_call_target="tpu_custom_call" | custom-call | tf_op jit(solution)/shard_map/adjoint_final/pallas_call | solution.py:616

commit v4 on v3

--- a/solution.py
+++ b/solution.py
@@ -334,7 +334,21 @@
 
     swap = [remote(design, design_beside, 0, 0, 1)]
     design_group = slabs(own_design, field)
+    corners = []
+    for q in (7, 8, 9, 10):
+        cx, cy, cz = velocity[q]
+        side, k, row = corner(q)
+        corners.append(
+            remote(
+                adjoint.at[q, 0 if cx > 0 else 15, slice(0, 1) if cy > 0 else slice(15, 16), :],
+                halo_x.at[side, k, row, :],
+                -cx,
+                -cy,
+                0,
+            )
+        )
     start(swap)
+    start(corners)
     start(design_group)
 
     z_faces = [
@@ -379,18 +393,6 @@
         remote(face_y.at[0], halo_y.at[0, :, 8:24, :], 0, 1, 0),
         remote(face_y.at[1], halo_y.at[1, :, 8:24, :], 0, -1, 0),
     ]
-    for q in (7, 8, 9, 10):
-        cx, cy, cz = velocity[q]
-        side, k, row = corner(q)
-        faces.append(
-            remote(
-                adjoint.at[q, 0 if cx > 0 else 15, slice(0, 1) if cy > 0 else slice(15, 16), :],
-                halo_x.at[side, k, row, :],
-                -cx,
-                -cy,
-                0,
-            )
-        )
     start(faces)
 
     loads[1].wait()
@@ -448,6 +450,7 @@
     source_own = chain[...] * lean[...]
     raw[...] = source_own
     own_side[...] = dot(source_own.reshape(256, 128), own_taps).reshape(16, 16, 128)
+    arrive(corners)
     arrive(faces)
 
     changes = []
@@ -552,7 +555,7 @@
 
     arrive(grad_group)
     arrive(edge_group)
-    for group in (design_group, faces, z_faces, swap, field_group, swap_raw, grad_group, edge_group):
+    for group in (design_group, corners, faces, z_faces, swap, field_group, swap_raw, grad_group, edge_group):
         sent(group)
 
 

time: 28.2 us -> 28.4 us (level); the launches traced: 28.1 us -> 27.9 us
  no operation moved by 1% of the time
where the time goes in v4:
time: 28.4 us; the launch traced here: 27.9 us
  Pallas kernels  27.3 us (96%)
  between operations  0.64 us (2%)
    pallas_call x1, Pallas kernels, local(): pl.pallas_call(main_kernel, out_shape=(vmem((Q,) + block), vmem(wide), vm...  25.7 us
    pallas_call x1, Pallas kernels, local(): pl.pallas_call(final_kernel, out_shape=(jax.ShapeDtypeStruct((Q,) + block...  1.58 us

profile of v4, /device:TPU:168, one launch (start us, length us, event | category | flops | bytes accessed | tf_op | source)
XLA Modules:
  0.0 27.9 jit_solution(8642097074193568316)
XLA Ops:
  0.6 25.7 %adjoint_main.1 = (f32[19,16,16,128]{3,2,1,0:T(8,128)S(1)}, f32[32,32,128]{2,1,0:T(8,128)S(1)}, f32[8,8,128]{2,1,0:T(8,128)S(1)}) custom-call(f32[19,16,16,128]{3,2,1,0:T(8,128)} %forward.1, f32[19,16,16,128]{3,2,1,0:T(8,128)} %adjoint.1, f32[16,16,128]{2,1,0:T(8,128)} %design.1, s32[16,16,128]{2,1,0:T(8,128)} %mask.1), custom_call_target="tpu_custom_call" | custom-call | tf_op jit(solution)/shard_map/adjoint_main/pallas_call | solution.py:581
  26.4 1.6 %adjoint_final.1 = (f32[19,16,16,128]{3,2,1,0:T(8,128)}, f32[16,16,128]{2,1,0:T(8,128)}) custom-call(f32[19,16,16,128]{3,2,1,0:T(8,128)S(1)} %get-tuple-element.5.next_in, f32[32,32,128]{2,1,0:T(8,128)S(1)} %get-tuple-element.6.grad, f32[8,8,128]{2,1,0:T(8,128)S(1)} %get-tuple-element.7.edges), custom_call_target="tpu_custom_call" | custom-call | tf_op jit(solution)/shard_map/adjoint_final/pallas_call | solution.py:619
